TPU v7x, 32 devices: a whole 2x2x4 slice. The times are simulated.
32 devices in a mesh: dp: 2 (over y), pipe: 4 (over x, core), seq: 4 (over z).
Axes of the slice: x: 2, y: 2, z: 4, core: 2. Of those that a mesh axis runs over, the one named last changes fastest.
Arguments:
- query_states: bfloat16 [8, 512, 8192], P(('dp', 'pipe'), 'seq'), parts along dimension 0, may hold values from -15 to 15
- projected_keys: bfloat16 [8, 512, 1024], P(('dp', 'pipe'), 'seq'), parts along dimension 0, may hold values from -8 to 8
- projected_values: bfloat16 [8, 512, 1024], P(('dp', 'pipe'), 'seq'), parts along dimension 0, may hold values from -6 to 6
- positions: int32 [8, 512], P(('dp', 'pipe'), 'seq'), parts along dimension 0, may hold values from 0 to 1023, as said below
- segments: int32 [8, 512], P(('dp', 'pipe'), 'seq'), parts along dimension 0, may hold values from 0 to 3, as said below
Outputs:
- handed: bfloat16 [8, 512, 8192], P(('dp', 'pipe'), 'seq'), parts along dimension 0
There are 2 independent parts, one for each index of `dp`. A program takes and returns all parts, laid end to end along the dimension named above; each array names one. Nothing has to cross between parts.
Inputs may be any that keep to these rules, and one draw needn't show every extreme that they name: `segments`: within each micro-batch ids never fall along the sequence, start at 0, every id occurs, and every document holds 4 or more tokens. `positions`: within a document a position is one more than the previous token's; the first document of each micro-batch starts at 0, and the last token of each micro-batch has position 1023.
All inputs are finite; a program needn't handle non-finite values.
Results may differ from a plain program's by a relative error of at most 0.0014.
The roundings to bfloat16 on the way count: a program that leaves them out, or rounds other values in their place, can miss the bound.
Values may be sent and summed in bfloat16 or wider, within the bound.
No kernel may reach another device: no remote copies, remote signals or barrier semaphores. Data moves between devices by JAX's collectives and lax.ppermute only.
A program may use at most 64 MiB of HBM per device.

v0:
```python
import functools
import math

import jax
import jax.numpy as jnp
from jax import lax
from jax.experimental import pallas as pl
from jax.experimental.pallas import tpu as pltpu
from jax.sharding import PartitionSpec as P


QUERY_HEADS = 64
KEY_VALUE_HEADS = 8
HEAD_SIZE = 128
GROUP = QUERY_HEADS // KEY_VALUE_HEADS
WIDTH = GROUP * HEAD_SIZE
SEGMENT_ROWS = 16
PAIR = 2
SMALL_LIMIT = 16 << 20

rope_theta = 1000000.0
yarn_factor = 4.0
trained_length = 32768.0
fast_beta = 32.0
slow_beta = 1.0
masked_score = -1e30


def yarn_frequencies(head_dim):
    half_dim = head_dim // 2
    pair_index = jnp.arange(half_dim, dtype=jnp.float32)
    base_freq = 1.0 / rope_theta ** (2.0 * pair_index / head_dim)
    lower = math.floor(
        head_dim
        * math.log(trained_length / (fast_beta * 2.0 * math.pi))
        / (2.0 * math.log(rope_theta))
    )
    upper = math.ceil(
        head_dim
        * math.log(trained_length / (slow_beta * 2.0 * math.pi))
        / (2.0 * math.log(rope_theta))
    )
    lower = max(lower, 0)
    upper = min(upper, head_dim - 1)
    upper = max(upper, lower + 1)
    ramp_value = jnp.clip((pair_index - lower) / (upper - lower), 0.0, 1.0)
    keep_share = 1.0 - ramp_value
    inv_freq = base_freq / yarn_factor * (1.0 - keep_share) + base_freq * keep_share
    return jnp.concatenate([inv_freq, inv_freq])[None]


def kept_in_hbm(array):
    return pltpu.with_memory_space_constraint(array, pltpu.HBM)


def rotated(states, cosine, sine):
    wide = states.astype(jnp.float32)
    return (wide * cosine + pltpu.roll(wide, HEAD_SIZE // 2, 1) * sine).astype(jnp.bfloat16)


def head_columns(g, width=HEAD_SIZE):
    return slice(g * width, (g + 1) * width)


def pack_kernel(chunks, rates_ref, *refs):
    packed = refs[4 : 4 + len(chunks)]
    cos_ref, sin_ref, positions_ref, segment_ref, keys_ref, values_ref, sems = refs[-7:]
    landed = (positions_ref, segment_ref, keys_ref, values_ref)
    arrivals = [
        pltpu.make_async_copy(source, target, sems.at[i])
        for i, (source, target) in enumerate(zip(refs[:4], landed))
    ]
    for copy in arrivals:
        copy.start()
    rows = keys_ref.shape[0]
    gain = 0.1 * math.log(yarn_factor) + 1.0
    arrivals[0].wait()
    tokens = positions_ref[...].astype(jnp.float32)
    angles = jnp.broadcast_to(tokens, (HEAD_SIZE, rows)).T * rates_ref[...]
    lane = lax.broadcasted_iota(jnp.int32, angles.shape, 1)
    cosine, sine = jnp.cos(angles) * gain, jnp.sin(angles) * gain
    sine = jnp.where(lane < HEAD_SIZE // 2, -sine, sine)
    cos_ref[...], sin_ref[...] = cosine, sine
    for copy in arrivals[1:]:
        copy.wait()
    ids = segment_ref[...].astype(jnp.float32).astype(jnp.bfloat16)
    first = 0
    for count, out_ref in zip(chunks, packed):
        for g in range(count):
            columns = head_columns(first + g)
            out_ref[g * rows : (g + 1) * rows, :] = rotated(keys_ref[:, columns], cosine, sine)
            out_ref[(count + g) * rows : (count + g + 1) * rows, :] = values_ref[:, columns]
        out_ref[2 * count * rows :, :] = jnp.broadcast_to(ids, (SEGMENT_ROWS, rows))
        first += count


def in_vmem(count):
    return [pl.BlockSpec(memory_space=pltpu.VMEM)] * count


def pack(chunks, positions, segments, keys, values):
    rows = keys.shape[0]
    tables = [jax.ShapeDtypeStruct((rows, HEAD_SIZE), jnp.float32)] * 2
    payloads = [
        jax.ShapeDtypeStruct((2 * count * rows + SEGMENT_ROWS, HEAD_SIZE), jnp.bfloat16)
        for count in chunks
    ]
    outs = pl.pallas_call(
        functools.partial(pack_kernel, chunks),
        in_specs=in_vmem(1) + [pl.BlockSpec(memory_space=pl.ANY)] * 4,
        out_specs=in_vmem(len(chunks) + 2),
        out_shape=payloads + tables,
        scratch_shapes=[
            *[pltpu.VMEM(x.shape, x.dtype) for x in (positions, segments, keys, values)],
            pltpu.SemaphoreType.DMA((4,)),
        ],
        compiler_params=pltpu.CompilerParams(vmem_limit_bytes=SMALL_LIMIT),
        name="pack",
        cost_estimate=pl.CostEstimate(
            flops=8 * keys.size, bytes_accessed=8 * keys.size, transcendentals=0
        ),
    )(yarn_frequencies(HEAD_SIZE), *map(kept_in_hbm, (positions, segments, keys, values)))
    return outs[:-2], outs[-2:]


def rotate_kernel(chunks, cos_ref, sin_ref, queries_hbm, *refs):
    outs, (queries_ref, sems) = refs[:-2], refs[-2:]
    cosine, sine = cos_ref[...], sin_ref[...]

    def arrival(g):
        source = queries_hbm.at[:, head_columns(g, WIDTH)]
        return pltpu.make_async_copy(source, queries_ref.at[g], sems.at[g])

    for g in range(sum(chunks)):
        arrival(g).start()
    first = 0
    for count, out_ref in zip(chunks, outs):
        for g in range(count):
            arrival(first + g).wait()
            for h in range(GROUP):
                states = queries_ref[first + g, :, head_columns(h)]
                out_ref[:, head_columns(g * GROUP + h)] = rotated(states, cosine, sine)
        first += count


def rotate(chunks, queries, tables):
    rows = queries.shape[0]
    return pl.pallas_call(
        functools.partial(rotate_kernel, chunks),
        in_specs=in_vmem(2) + [pl.BlockSpec(memory_space=pl.ANY)],
        out_specs=in_vmem(len(chunks)),
        out_shape=[jax.ShapeDtypeStruct((rows, n * WIDTH), jnp.bfloat16) for n in chunks],
        scratch_shapes=[
            pltpu.VMEM((sum(chunks), rows, WIDTH), jnp.bfloat16),
            pltpu.SemaphoreType.DMA((sum(chunks),)),
        ],
        compiler_params=pltpu.CompilerParams(vmem_limit_bytes=SMALL_LIMIT),
        name="rotate",
        cost_estimate=pl.CostEstimate(
            flops=4 * queries.size, bytes_accessed=4 * queries.size, transcendentals=0
        ),
    )(*tables, kept_in_hbm(queries))


def attend_kernel(first, count, size, here_ref, queries_ref, *refs):
    payloads = refs[:size]
    out_hbm, bias_ref, out_ref, sems = refs[-4:]
    rows = queries_ref.shape[0]

    def departure(g):
        start = (first + g) * WIDTH
        start = start if isinstance(g, int) else pl.multiple_of(start, WIDTH)
        target = out_hbm.at[:, pl.ds(start, WIDTH)]
        return pltpu.make_async_copy(out_ref.at[g], target, sems.at[g])

    def ids_of(hop):
        ids = payloads[hop][2 * count * rows : 2 * count * rows + SEGMENT_ROWS, :]
        return jnp.broadcast_to(ids.astype(jnp.float32)[0:1, :], (rows, rows))

    here = here_ref[0]
    query_ids = ids_of(0).T
    row = lax.broadcasted_iota(jnp.int32, (rows, rows), 0)
    lane = lax.broadcasted_iota(jnp.int32, (rows, rows), 1)
    for hop in range(size):
        ahead = jnp.where(here >= hop, -hop * rows, (size - hop) * rows)
        visible = (query_ids == ids_of(hop)) & (lane + ahead <= row)
        bias_ref[:, hop * rows : (hop + 1) * rows] = jnp.where(visible, 0.0, masked_score)

    rate = math.log2(math.e) / math.sqrt(HEAD_SIZE)

    def heads_of(i):
        return range(i * PAIR, (i + 1) * PAIR)

    def attend_group(g, carry):
        def gathered(start):
            start = pl.multiple_of(start * rows, rows)
            return jnp.concatenate([p[pl.ds(start, rows), :] for p in payloads], axis=0)

        keys = gathered(g)
        values = gathered(count + g)

        def scored(i):
            heads = [pl.multiple_of(g * WIDTH + h * HEAD_SIZE, HEAD_SIZE) for h in heads_of(i)]
            return lax.dot_general(
                jnp.concatenate([queries_ref[:, pl.ds(h, HEAD_SIZE)] for h in heads], axis=0),
                keys,
                (((1,), (1,)), ((), ())),
                preferred_element_type=jnp.float32,
            )

        def finish(i, rounded, totals):
            summed = jnp.dot(rounded, values, preferred_element_type=jnp.float32)
            result = (summed / totals).astype(jnp.bfloat16)
            for k, h in enumerate(heads_of(i)):
                out_ref[g, :, head_columns(h)] = result[k * rows : (k + 1) * rows]

        following = scored(0)
        waiting = None
        for i in range(GROUP // PAIR):
            scores = following
            if i + 1 < GROUP // PAIR:
                following = scored(i + 1)
            if waiting is not None:
                finish(*waiting)
            scores = scores.reshape(PAIR, rows, -1) + bias_ref[...][None]
            scores = scores.reshape(PAIR * rows, -1)
            best = jnp.max(scores, axis=1, keepdims=True)
            weights = jnp.exp2((scores - best) * rate)
            totals = jnp.sum(weights, axis=1, keepdims=True)
            waiting = (i, weights.astype(jnp.bfloat16), totals)
        finish(*waiting)
        departure(g).start()
        return carry

    lax.fori_loop(0, count, attend_group, 0)
    for g in range(count):
        departure(g).wait()


def attend(queries, held, here, first=0, onto=None):
    rows = queries.shape[0]
    count = queries.shape[1] // WIDTH
    size = len(held)
    keys = size * rows
    so_far = [] if onto is None else [onto]
    hbm = pl.BlockSpec(memory_space=pl.ANY)
    return pl.pallas_call(
        functools.partial(attend_kernel, first, count, size),
        in_specs=[pl.BlockSpec(memory_space=pltpu.SMEM)] + in_vmem(1 + size) + [hbm] * len(so_far),
        out_specs=hbm,
        out_shape=jax.ShapeDtypeStruct((rows, KEY_VALUE_HEADS * WIDTH), jnp.bfloat16),
        scratch_shapes=[
            pltpu.VMEM((rows, keys), jnp.float32),
            pltpu.VMEM((count, rows, WIDTH), jnp.bfloat16),
            pltpu.SemaphoreType.DMA((count,)),
        ],
        input_output_aliases={2 + size: 0} if so_far else {},
        compiler_params=pltpu.CompilerParams(vmem_limit_bytes=(12 << 20) + 9216 * keys),
        name="attend",
        cost_estimate=pl.CostEstimate(
            flops=4 * rows * keys * count * WIDTH,
            bytes_accessed=4 * rows * count * WIDTH,
            transcendentals=rows * keys * count * GROUP,
        ),
    )(here, queries, *held, *so_far)


def ring(block, axis):
    size = lax.axis_size(axis)
    return lax.ppermute(block, axis, [(i, (i + 1) % size) for i in range(size)])


def ring_both(block):
    sections, size = lax.axis_size("pipe"), lax.axis_size("seq")
    route = [
        (p * size + z, (p + 1) % sections * size + (z + 1) % size)
        for p in range(sections)
        for z in range(size)
    ]
    return lax.ppermute(block, ("pipe", "seq"), route)


CHUNKS = (2, 3, 3)


def on_device(query_states, projected_keys, projected_values, positions, segments):
    here = lax.axis_index("seq").astype(jnp.int32).reshape(1)
    size = lax.axis_size("seq")
    firsts = [sum(CHUNKS[:c]) for c in range(len(CHUNKS))]
    packed, tables = pack(CHUNKS, positions, segments, projected_keys[0], projected_values[0])
    held = []
    for c, payload in enumerate(packed):
        blocks = [ring(payload, "pipe")]
        for hop in range(1, size):
            both = hop == 1 and c in DIAGONAL
            blocks.append(ring_both(payload) if both else ring(blocks[-1], "seq"))
        held.append(blocks)
    turned = rotate(CHUNKS, query_states[0], tables)
    out = None
    for c in range(len(CHUNKS)):
        queries = ring(turned[c], "pipe")
        out = attend(queries, held[c], here, firsts[c], out)
    return out[None]


DIAGONAL = (0, 1, 2)


def solution(mesh):
    placed = (
        P(("dp", "pipe"), "seq", None),
        P(("dp", "pipe"), "seq", None),
        P(("dp", "pipe"), "seq", None),
        P(("dp", "pipe"), "seq"),
        P(("dp", "pipe"), "seq"),
    )
    return jax.shard_map(
        on_device,
        mesh=mesh,
        in_specs=placed,
        out_specs=P(("dp", "pipe"), "seq", None),
        check_vma=False,
    )
```

profile of v0, /device:TPU:0, one launch (start us, length us, event | category | flops | bytes accessed | tf_op | source)
XLA Modules:
  0.0 62.9 jit_solution(4877628060780119912)
XLA Ops:
  0.0 0.1 maximum_bitcast_fusion.rates_ref
  0.1 2.0 %pack.1 = (bf16[528,128]{1,0:T(8,128)(2,1)S(1)}, bf16[784,128]{1,0:T(8,128)(2,1)S(1)}, bf16[784,128]{1,0:T(8,128)(2,1)}, f32[128,128]{1,0:T(8,128)S(1)}, f32[128,128]{1,0:T(8,128)S(1)}) custom-call(f32[1,128]{1,0:T(1,128)S(1)} %maximum_bitcast_fusion.rates_ref, s32[1,128]{1,0:T(1,128)} %refs_0_.1, s32[1,128]{1,0:T(1,128)} %refs_1_.1, ...), custom_call_target="tpu_custom_call" | custom-call | flops 1048576 | bytes 1048576 | tf_op jit(solution)/shard_map/pack/pallas_call | solution.py:108
  2.1 2.5 %collective-permute-start.7 = (bf16[784,128]{1,0:T(8,128)(2,1)S(1)}, bf16[784,128]{1,0:T(8,128)(2,1)S(1)}, u32[]{:S(2)}, u32[]{:S(2)}) collective-permute-start(bf16[784,128]{1,0:T(8,128)(2,1)S(1)} %get-tuple-element.18), channel_id=1, source_target_pairs={{0,5},{1,6},{2,7},{3,4},{4,9},{5,10},{6,11},{7,8},{8,13},{9,14},{1... | collective-permute-start | bytes 602120 | tf_op jit(solution)/shard_map/ppermute | solution.py:280
  4.6 2.8 %collective-permute-start.12 = (bf16[528,128]{1,0:T(8,128)(2,1)S(1)}, bf16[528,128]{1,0:T(8,128)(2,1)S(1)}, u32[]{:S(2)}, u32[]{:S(2)}) collective-permute-start(bf16[528,128]{1,0:T(8,128)(2,1)S(1)} %get-tuple-element.20), channel_id=1, source_target_pairs={{0,5},{1,6},{2,7},{3,4},{4,9},{5,10},{6,11},{7,8},{8,13},{9,14},{1... | collective-permute-start | bytes 405512 | tf_op jit(solution)/shard_map/ppermute | solution.py:280
  7.4 3.4 %rotate.1 = (bf16[128,2048]{1,0:T(8,128)(2,1)S(1)}, bf16[128,3072]{1,0:T(8,128)(2,1)}, bf16[128,3072]{1,0:T(8,128)(2,1)}) custom-call(f32[128,128]{1,0:T(8,128)S(1)} %get-tuple-element.13.cos_ref, f32[128,128]{1,0:T(8,128)S(1)} %get-tuple-element.14.sin_ref, bf16[128,8192]{1,0:T(8,128)(2,1)} %bitcast.7), custom_call_target="tpu_custom_call" | custom-call | flops 4194304 | bytes 4194304 | tf_op jit(solution)/shard_map/rotate/pallas_call | solution.py:148
  10.8 0.7 %collective-permute-start.5 = (bf16[128,3072]{1,0:T(8,128)(2,1)}, bf16[128,3072]{1,0:T(8,128)(2,1)S(1)}, u32[]{:S(2)}, u32[]{:S(2)}) collective-permute-start(bf16[128,3072]{1,0:T(8,128)(2,1)} %get-tuple-element.17), channel_id=1, source_target_pairs={{0,4},{4,8},{8,12},{12,0},{1,5},{5,9},{9,13},{13,1},{2,6},{6,10},{... | collective-permute-start | bytes 2359304 | tf_op jit(solution)/shard_map/ppermute | solution.py:270
  11.5 0.1 collective-permute-start.6
  11.6 3.6 %collective-permute-done.12.refs_1_ = bf16[528,128]{1,0:T(8,128)(2,1)S(1)} collective-permute-done((bf16[528,128]{1,0:T(8,128)(2,1)S(1)}, bf16[528,128]{1,0:T(8,128)(2,1)S(1)}, u32[]{:S(2)}, u32[]{:S(2)}) %collective-permute-start.12) | collective-permute-done | bytes 135200 | tf_op jit(solution)/shard_map/ppermute | solution.py:280
  15.2 0.1 collective-permute-start
  15.3 0.0 collective-permute-done.11.refs_0_
  15.3 0.7 %copy-done.2 = bf16[528,128]{1,0:T(8,128)(2,1)} copy-done((bf16[528,128]{1,0:T(8,128)(2,1)}, bf16[528,128]{1,0:T(8,128)(2,1)S(1)}, u32[]{:S(2)}) %copy-start.2) | copy-done | bytes 135192
  15.9 1.4 %collective-permute-start.2 = (bf16[784,128]{1,0:T(8,128)(2,1)}, bf16[784,128]{1,0:T(8,128)(2,1)S(1)}, u32[]{:S(2)}, u32[]{:S(2)}) collective-permute-start(bf16[784,128]{1,0:T(8,128)(2,1)} %get-tuple-element.16), channel_id=1, source_target_pairs={{0,5},{1,6},{2,7},{3,4},{4,9},{5,10},{6,11},{7,8},{8,13},{9,14},{1... | collective-permute-start | bytes 602120 | tf_op jit(solution)/shard_map/ppermute | solution.py:280
  17.3 0.0 collective-permute-done.7.refs_1_
  17.3 1.0 %collective-permute-start.10 = (bf16[128,2048]{1,0:T(8,128)(2,1)S(1)}, bf16[128,2048]{1,0:T(8,128)(2,1)S(1)}, u32[]{:S(2)}, u32[]{:S(2)}) collective-permute-start(bf16[128,2048]{1,0:T(8,128)(2,1)S(1)} %get-tuple-element.19), channel_id=1, source_target_pairs={{0,4},{4,8},{8,12},{12,0},{1,5},{5,9},{9,13},{13,1},{2,6},{6,10},{... | collective-permute-start | bytes 1572872 | tf_op jit(solution)/shard_map/ppermute | solution.py:270
  18.3 9.0 %collective-permute-done.6.refs_0_ = bf16[784,128]{1,0:T(8,128)(2,1)S(1)} collective-permute-done((bf16[784,128]{1,0:T(8,128)(2,1)S(1)}, bf16[784,128]{1,0:T(8,128)(2,1)S(1)}, u32[]{:S(2)}, u32[]{:S(2)}) %collective-permute-start.6) | collective-permute-done | bytes 200736 | tf_op jit(solution)/shard_map/ppermute | solution.py:270
  27.3 1.3 %collective-permute-start.13 = (bf16[528,128]{1,0:T(8,128)(2,1)S(1)}, bf16[528,128]{1,0:T(8,128)(2,1)S(1)}, u32[]{:S(2)}, u32[]{:S(2)}) collective-permute-start(bf16[528,128]{1,0:T(8,128)(2,1)S(1)} %collective-permute-done.12.refs_1_), channel_id=1, source_target_pairs={{0,1},{1,2},{2,3},{3,0},{4,5},{5,6},{6,7},{7,4},{8,9},{9,10},{10,1... | collective-permute-start | bytes 405512 | tf_op jit(solution)/shard_map/ppermute | solution.py:270
  28.6 0.7 %copy-done = bf16[528,128]{1,0:T(8,128)(2,1)} copy-done((bf16[528,128]{1,0:T(8,128)(2,1)}, bf16[528,128]{1,0:T(8,128)(2,1)S(1)}, u32[]{:S(2)}) %copy-start) | copy-done | bytes 135192
  29.3 0.0 collective-permute-done.2.refs_1_
  29.3 1.0 %collective-permute-start.8 = (bf16[784,128]{1,0:T(8,128)(2,1)S(1)}, bf16[784,128]{1,0:T(8,128)(2,1)S(1)}, u32[]{:S(2)}, u32[]{:S(2)}) collective-permute-start(bf16[784,128]{1,0:T(8,128)(2,1)S(1)} %collective-permute-done.7.refs_1_), channel_id=1, source_target_pairs={{0,1},{1,2},{2,3},{3,0},{4,5},{5,6},{6,7},{7,4},{8,9},{9,10},{10,1... | collective-permute-start | bytes 602120 | tf_op jit(solution)/shard_map/ppermute | solution.py:270
  30.3 5.3 %collective-permute-done.13.refs_2_ = bf16[528,128]{1,0:T(8,128)(2,1)S(1)} collective-permute-done((bf16[528,128]{1,0:T(8,128)(2,1)S(1)}, bf16[528,128]{1,0:T(8,128)(2,1)S(1)}, u32[]{:S(2)}, u32[]{:S(2)}) %collective-permute-start.13) | collective-permute-done | bytes 135200 | tf_op jit(solution)/shard_map/ppermute | solution.py:270
  35.6 4.2 %collective-permute-done.8.refs_2_ = bf16[784,128]{1,0:T(8,128)(2,1)S(1)} collective-permute-done((bf16[784,128]{1,0:T(8,128)(2,1)S(1)}, bf16[784,128]{1,0:T(8,128)(2,1)S(1)}, u32[]{:S(2)}, u32[]{:S(2)}) %collective-permute-start.8) | collective-permute-done | bytes 200736 | tf_op jit(solution)/shard_map/ppermute | solution.py:270
  39.8 0.6 %copy-done.4 = bf16[528,128]{1,0:T(8,128)(2,1)} copy-done((bf16[528,128]{1,0:T(8,128)(2,1)}, bf16[528,128]{1,0:T(8,128)(2,1)S(1)}, u32[]{:S(2)}) %copy-start.4) | copy-done | bytes 135192
  40.4 4.1 %collective-permute-done.3.refs_2_ = bf16[784,128]{1,0:T(8,128)(2,1)S(1)} collective-permute-done((bf16[784,128]{1,0:T(8,128)(2,1)S(1)}, bf16[784,128]{1,0:T(8,128)(2,1)S(1)}, u32[]{:S(2)}, u32[]{:S(2)}) %collective-permute-start.3) | collective-permute-done | bytes 200736 | tf_op jit(solution)/shard_map/ppermute | solution.py:270
  44.5 3.5 %collective-permute-done.14.refs_3_ = bf16[528,128]{1,0:T(8,128)(2,1)S(1)} collective-permute-done((bf16[528,128]{1,0:T(8,128)(2,1)S(1)}, bf16[528,128]{1,0:T(8,128)(2,1)S(1)}, u32[]{:S(2)}, u32[]{:S(2)}) %collective-permute-start.14) | collective-permute-done | bytes 135200 | tf_op jit(solution)/shard_map/ppermute | solution.py:270
  48.0 0.7 %copy-done.6 = bf16[528,128]{1,0:T(8,128)(2,1)} copy-done((bf16[528,128]{1,0:T(8,128)(2,1)}, bf16[528,128]{1,0:T(8,128)(2,1)S(1)}, u32[]{:S(2)}) %copy-start.6) | copy-done | bytes 135192
  48.7 0.9 %copy-done.1 = bf16[528,128]{1,0:T(8,128)(2,1)S(1)} copy-done((bf16[528,128]{1,0:T(8,128)(2,1)S(1)}, bf16[528,128]{1,0:T(8,128)(2,1)}, u32[]{:S(2)}) %copy-start.1) | copy-done | bytes 135192
  49.6 0.9 %copy-done.3 = bf16[528,128]{1,0:T(8,128)(2,1)S(1)} copy-done((bf16[528,128]{1,0:T(8,128)(2,1)S(1)}, bf16[528,128]{1,0:T(8,128)(2,1)}, u32[]{:S(2)}) %copy-start.3) | copy-done | bytes 135192
  50.5 0.9 %copy-done.5 = bf16[528,128]{1,0:T(8,128)(2,1)S(1)} copy-done((bf16[528,128]{1,0:T(8,128)(2,1)S(1)}, bf16[528,128]{1,0:T(8,128)(2,1)}, u32[]{:S(2)}) %copy-start.5) | copy-done | bytes 135192
  51.4 0.9 %copy-done.7 = bf16[528,128]{1,0:T(8,128)(2,1)S(1)} copy-done((bf16[528,128]{1,0:T(8,128)(2,1)S(1)}, bf16[528,128]{1,0:T(8,128)(2,1)}, u32[]{:S(2)}) %copy-start.7) | copy-done | bytes 135192
  52.3 2.6 %attend.3.refs_4_ = bf16[128,8192]{1,0:T(8,128)(2,1)} custom-call(s32[1]{0:T(128)} %bitcast.here_ref, bf16[128,2048]{1,0:T(8,128)(2,1)S(1)} %collective-permute-done.10.queries_ref, bf16[528,128]{1,0:T(8,128)(2,1)S(1)} %copy-done.3, bf16[528,128]{1,0:T(8,128)(2,1)S(1)} %copy-done.1, bf16[528,128]{1,0:T(8,128)(2,1)S(1)} %copy-done.5, ...), custom_call_target="tpu_custom_call" | custom-call | flops 536870912 | bytes 1048576 | tf_op jit(solution)/shard_map/attend/pallas_call | solution.py:247
  55.0 4.4 %attend.4.refs_4_ = bf16[128,8192]{1,0:T(8,128)(2,1)} custom-call(s32[1]{0:T(128)} %bitcast.here_ref, bf16[128,3072]{1,0:T(8,128)(2,1)S(1)} %collective-permute-done.5.queries_ref, bf16[784,128]{1,0:T(8,128)(2,1)S(1)} %collective-permute-done.6.refs_0_, bf16[784,128]{1,0:T(8,128)(2,1)S(1)} %collective-permute-done.7.refs_1_, ...), custom_call_target="tpu_custom_call", output_to_operand_aliasing={{}: (6, {})} | custom-call | flops 805306368 | bytes 1572864 | tf_op jit(solution)/shard_map/attend/pallas_call | solution.py:247
  59.4 3.5 %attend.5 = bf16[128,8192]{1,0:T(8,128)(2,1)} custom-call(s32[1]{0:T(128)} %bitcast.here_ref, bf16[128,3072]{1,0:T(8,128)(2,1)S(1)} %collective-permute-done.queries_ref, bf16[784,128]{1,0:T(8,128)(2,1)S(1)} %collective-permute-done.1.refs_0_, bf16[784,128]{1,0:T(8,128)(2,1)S(1)} %collective-permute-done.2.refs_1_, ...), custom_call_target="tpu_custom_call", output_to_operand_aliasing={{}: (6, {})} | custom-call | flops 805306368 | bytes 1572864 | tf_op jit(solution)/shard_map/attend/pallas_call | solution.py:247
  (21 shorter events, 0.1 us)
Async XLA Ops:
  2.1 15.2 %collective-permute-start.7 = (bf16[784,128]{1,0:T(8,128)(2,1)S(1)}, bf16[784,128]{1,0:T(8,128)(2,1)S(1)}, u32[]{:S(2)}, u32[]{:S(2)}) collective-permute-start(bf16[784,128]{1,0:T(8,128)(2,1)S(1)} %get-tuple-element.18), channel_id=1, source_target_pairs={{0,5},{1,6},{2,7},{3,4},{4,9},{5,10},{6,11},{7,8},{8,13},{9,14},{1... | collective-permute-start | bytes 602120 | tf_op jit(solution)/shard_map/ppermute | solution.py:280
  4.6 10.5 %collective-permute-start.12 = (bf16[528,128]{1,0:T(8,128)(2,1)S(1)}, bf16[528,128]{1,0:T(8,128)(2,1)S(1)}, u32[]{:S(2)}, u32[]{:S(2)}) collective-permute-start(bf16[528,128]{1,0:T(8,128)(2,1)S(1)} %get-tuple-element.20), channel_id=1, source_target_pairs={{0,5},{1,6},{2,7},{3,4},{4,9},{5,10},{6,11},{7,8},{8,13},{9,14},{1... | collective-permute-start | bytes 405512 | tf_op jit(solution)/shard_map/ppermute | solution.py:280
  7.4 7.9 %collective-permute-start.11 = (bf16[528,128]{1,0:T(8,128)(2,1)S(1)}, bf16[528,128]{1,0:T(8,128)(2,1)S(1)}, u32[]{:S(2)}, u32[]{:S(2)}) collective-permute-start(bf16[528,128]{1,0:T(8,128)(2,1)S(1)} %get-tuple-element.20), channel_id=1, source_target_pairs={{0,4},{4,8},{8,12},{12,0},{1,5},{5,9},{9,13},{13,1},{2,6},{6,10},{... | collective-permute-start | bytes 405512 | tf_op jit(solution)/shard_map/ppermute | solution.py:270
  10.8 44.2 %collective-permute-start.5 = (bf16[128,3072]{1,0:T(8,128)(2,1)}, bf16[128,3072]{1,0:T(8,128)(2,1)S(1)}, u32[]{:S(2)}, u32[]{:S(2)}) collective-permute-start(bf16[128,3072]{1,0:T(8,128)(2,1)} %get-tuple-element.17), channel_id=1, source_target_pairs={{0,4},{4,8},{8,12},{12,0},{1,5},{5,9},{9,13},{13,1},{2,6},{6,10},{... | collective-permute-start | bytes 2359304 | tf_op jit(solution)/shard_map/ppermute | solution.py:270
  11.5 15.8 %collective-permute-start.6 = (bf16[784,128]{1,0:T(8,128)(2,1)S(1)}, bf16[784,128]{1,0:T(8,128)(2,1)S(1)}, u32[]{:S(2)}, u32[]{:S(2)}) collective-permute-start(bf16[784,128]{1,0:T(8,128)(2,1)S(1)} %get-tuple-element.18), channel_id=1, source_target_pairs={{0,4},{4,8},{8,12},{12,0},{1,5},{5,9},{9,13},{13,1},{2,6},{6,10},{... | collective-permute-start | bytes 602120 | tf_op jit(solution)/shard_map/ppermute | solution.py:270
  15.2 44.2 %collective-permute-start = (bf16[128,3072]{1,0:T(8,128)(2,1)}, bf16[128,3072]{1,0:T(8,128)(2,1)S(1)}, u32[]{:S(2)}, u32[]{:S(2)}) collective-permute-start(bf16[128,3072]{1,0:T(8,128)(2,1)} %get-tuple-element.15), channel_id=1, source_target_pairs={{0,4},{4,8},{8,12},{12,0},{1,5},{5,9},{9,13},{13,1},{2,6},{6,10},{... | collective-permute-start | bytes 2359304 | tf_op jit(solution)/shard_map/ppermute | solution.py:270
  15.3 0.7 %copy-start.2 = (bf16[528,128]{1,0:T(8,128)(2,1)}, bf16[528,128]{1,0:T(8,128)(2,1)S(1)}, u32[]{:S(2)}) copy-start(bf16[528,128]{1,0:T(8,128)(2,1)S(1)} %collective-permute-done.11.refs_0_) | copy-start | bytes 405508
  15.9 13.4 %collective-permute-start.2 = (bf16[784,128]{1,0:T(8,128)(2,1)}, bf16[784,128]{1,0:T(8,128)(2,1)S(1)}, u32[]{:S(2)}, u32[]{:S(2)}) collective-permute-start(bf16[784,128]{1,0:T(8,128)(2,1)} %get-tuple-element.16), channel_id=1, source_target_pairs={{0,5},{1,6},{2,7},{3,4},{4,9},{5,10},{6,11},{7,8},{8,13},{9,14},{1... | collective-permute-start | bytes 602120 | tf_op jit(solution)/shard_map/ppermute | solution.py:280
  17.3 31.4 %collective-permute-start.10 = (bf16[128,2048]{1,0:T(8,128)(2,1)S(1)}, bf16[128,2048]{1,0:T(8,128)(2,1)S(1)}, u32[]{:S(2)}, u32[]{:S(2)}) collective-permute-start(bf16[128,2048]{1,0:T(8,128)(2,1)S(1)} %get-tuple-element.19), channel_id=1, source_target_pairs={{0,4},{4,8},{8,12},{12,0},{1,5},{5,9},{9,13},{13,1},{2,6},{6,10},{... | collective-permute-start | bytes 1572872 | tf_op jit(solution)/shard_map/ppermute | solution.py:270
  27.3 8.3 %collective-permute-start.13 = (bf16[528,128]{1,0:T(8,128)(2,1)S(1)}, bf16[528,128]{1,0:T(8,128)(2,1)S(1)}, u32[]{:S(2)}, u32[]{:S(2)}) collective-permute-start(bf16[528,128]{1,0:T(8,128)(2,1)S(1)} %collective-permute-done.12.refs_1_), channel_id=1, source_target_pairs={{0,1},{1,2},{2,3},{3,0},{4,5},{5,6},{6,7},{7,4},{8,9},{9,10},{10,1... | collective-permute-start | bytes 405512 | tf_op jit(solution)/shard_map/ppermute | solution.py:270
  28.6 0.7 %copy-start = (bf16[528,128]{1,0:T(8,128)(2,1)}, bf16[528,128]{1,0:T(8,128)(2,1)S(1)}, u32[]{:S(2)}) copy-start(bf16[528,128]{1,0:T(8,128)(2,1)S(1)} %collective-permute-done.12.refs_1_) | copy-start | bytes 405508
  29.3 10.5 %collective-permute-start.8 = (bf16[784,128]{1,0:T(8,128)(2,1)S(1)}, bf16[784,128]{1,0:T(8,128)(2,1)S(1)}, u32[]{:S(2)}, u32[]{:S(2)}) collective-permute-start(bf16[784,128]{1,0:T(8,128)(2,1)S(1)} %collective-permute-done.7.refs_1_), channel_id=1, source_target_pairs={{0,1},{1,2},{2,3},{3,0},{4,5},{5,6},{6,7},{7,4},{8,9},{9,10},{10,1... | collective-permute-start | bytes 602120 | tf_op jit(solution)/shard_map/ppermute | solution.py:270
  35.6 9.0 %collective-permute-start.3 = (bf16[784,128]{1,0:T(8,128)(2,1)S(1)}, bf16[784,128]{1,0:T(8,128)(2,1)S(1)}, u32[]{:S(2)}, u32[]{:S(2)}) collective-permute-start(bf16[784,128]{1,0:T(8,128)(2,1)S(1)} %collective-permute-done.2.refs_1_), channel_id=1, source_target_pairs={{0,1},{1,2},{2,3},{3,0},{4,5},{5,6},{6,7},{7,4},{8,9},{9,10},{10,1... | collective-permute-start | bytes 602120 | tf_op jit(solution)/shard_map/ppermute | solution.py:270
  39.8 8.3 %collective-permute-start.14 = (bf16[528,128]{1,0:T(8,128)(2,1)S(1)}, bf16[528,128]{1,0:T(8,128)(2,1)S(1)}, u32[]{:S(2)}, u32[]{:S(2)}) collective-permute-start(bf16[528,128]{1,0:T(8,128)(2,1)S(1)} %collective-permute-done.13.refs_2_), channel_id=1, source_target_pairs={{0,1},{1,2},{2,3},{3,0},{4,5},{5,6},{6,7},{7,4},{8,9},{9,10},{10,1... | collective-permute-start | bytes 405512 | tf_op jit(solution)/shard_map/ppermute | solution.py:270
  39.8 0.6 %copy-start.4 = (bf16[528,128]{1,0:T(8,128)(2,1)}, bf16[528,128]{1,0:T(8,128)(2,1)S(1)}, u32[]{:S(2)}) copy-start(bf16[528,128]{1,0:T(8,128)(2,1)S(1)} %collective-permute-done.13.refs_2_) | copy-start | bytes 405508
  44.5 10.4 %collective-permute-start.9 = (bf16[784,128]{1,0:T(8,128)(2,1)S(1)}, bf16[784,128]{1,0:T(8,128)(2,1)}, u32[]{:S(2)}, u32[]{:S(2)}) collective-permute-start(bf16[784,128]{1,0:T(8,128)(2,1)S(1)} %collective-permute-done.8.refs_2_), channel_id=1, source_target_pairs={{0,1},{1,2},{2,3},{3,0},{4,5},{5,6},{6,7},{7,4},{8,9},{9,10},{10,1... | collective-permute-start | bytes 602120 | tf_op jit(solution)/shard_map/ppermute | solution.py:270
  48.0 0.7 %copy-start.6 = (bf16[528,128]{1,0:T(8,128)(2,1)}, bf16[528,128]{1,0:T(8,128)(2,1)S(1)}, u32[]{:S(2)}) copy-start(bf16[528,128]{1,0:T(8,128)(2,1)S(1)} %collective-permute-done.14.refs_3_) | copy-start | bytes 405508
  48.7 10.7 %collective-permute-start.1 = (bf16[784,128]{1,0:T(8,128)(2,1)}, bf16[784,128]{1,0:T(8,128)(2,1)S(1)}, u32[]{:S(2)}, u32[]{:S(2)}) collective-permute-start(bf16[784,128]{1,0:T(8,128)(2,1)} %get-tuple-element.16), channel_id=1, source_target_pairs={{0,4},{4,8},{8,12},{12,0},{1,5},{5,9},{9,13},{13,1},{2,6},{6,10},{... | collective-permute-start | bytes 602120 | tf_op jit(solution)/shard_map/ppermute | solution.py:270
  48.7 10.7 %collective-permute-start.4 = (bf16[784,128]{1,0:T(8,128)(2,1)S(1)}, bf16[784,128]{1,0:T(8,128)(2,1)S(1)}, u32[]{:S(2)}, u32[]{:S(2)}) collective-permute-start(bf16[784,128]{1,0:T(8,128)(2,1)S(1)} %collective-permute-done.3.refs_2_), channel_id=1, source_target_pairs={{0,1},{1,2},{2,3},{3,0},{4,5},{5,6},{6,7},{7,4},{8,9},{9,10},{10,1... | collective-permute-start | bytes 602120 | tf_op jit(solution)/shard_map/ppermute | solution.py:270
  48.7 0.9 %copy-start.1 = (bf16[528,128]{1,0:T(8,128)(2,1)S(1)}, bf16[528,128]{1,0:T(8,128)(2,1)}, u32[]{:S(2)}) copy-start(bf16[528,128]{1,0:T(8,128)(2,1)} %copy-done) | copy-start | bytes 405508
  49.6 0.9 %copy-start.3 = (bf16[528,128]{1,0:T(8,128)(2,1)S(1)}, bf16[528,128]{1,0:T(8,128)(2,1)}, u32[]{:S(2)}) copy-start(bf16[528,128]{1,0:T(8,128)(2,1)} %copy-done.2) | copy-start | bytes 405508
  50.5 0.9 %copy-start.5 = (bf16[528,128]{1,0:T(8,128)(2,1)S(1)}, bf16[528,128]{1,0:T(8,128)(2,1)}, u32[]{:S(2)}) copy-start(bf16[528,128]{1,0:T(8,128)(2,1)} %copy-done.4) | copy-start | bytes 405508
  51.4 0.9 %copy-start.7 = (bf16[528,128]{1,0:T(8,128)(2,1)S(1)}, bf16[528,128]{1,0:T(8,128)(2,1)}, u32[]{:S(2)}) copy-start(bf16[528,128]{1,0:T(8,128)(2,1)} %copy-done.6) | copy-start | bytes 405508
where the time goes:
time: 63.6 us; the launch traced here: 62.9 us
  waiting for transfers between devices  29.7 us (47%)
  Pallas kernels  15.9 us (25%)
  starting transfers between devices  10.9 us (17%)
  local copies, waits for them, and re-layouts  6.22 us (10%)
    ppermute x12, waiting for transfers between devices, ring(): return lax.ppermute(block, axis, [(i, (i + 1) % size) for i in range(size)])  26.1 us
    pallas_call x3, Pallas kernels, attend(): pl.pallas_call(functools.partial(attend_kernel, first, count, size), in_s...  10.5 us
    ppermute x3, starting transfers between devices, ring_both(): return lax.ppermute(block, ('pipe', 'seq'), route)  6.68 us
    unnamed x16, local copies, waits for them, and re-layouts  6.22 us
    ppermute x12, starting transfers between devices, ring(): return lax.ppermute(block, axis, [(i, (i + 1) % size) for i in range(size)])  4.22 us
    ppermute x3, waiting for transfers between devices, ring_both(): return lax.ppermute(block, ('pipe', 'seq'), route)  3.6 us
    pallas_call x1, Pallas kernels, rotate(): pl.pallas_call(functools.partial(rotate_kernel, chunks), in_specs=in_vmem...  3.39 us
    pallas_call x1, Pallas kernels, pack(): pl.pallas_call(functools.partial(pack_kernel, chunks), in_specs=in_vmem(1...  1.97 us
  transfers between devices with their start and end apart: 15, of which 6 were waited for; matrix products, arithmetic and copies ran while one was open for 0% of the time, Pallas kernels for 17%

commit v1 on v0

--- a/solution.py
+++ b/solution.py
@@ -164,7 +164,10 @@
 
 def attend_kernel(first, count, size, here_ref, queries_ref, *refs):
     payloads = refs[:size]
-    out_hbm, bias_ref, out_ref, sems = refs[-4:]
+    if first is None:
+        out_ref, bias_ref = refs[-2:]
+    else:
+        out_hbm, bias_ref, out_ref, sems = refs[-4:]
     rows = queries_ref.shape[0]
 
     def departure(g):
@@ -229,31 +232,38 @@
             totals = jnp.sum(weights, axis=1, keepdims=True)
             waiting = (i, weights.astype(jnp.bfloat16), totals)
         finish(*waiting)
-        departure(g).start()
+        if first is not None:
+            departure(g).start()
         return carry
 
     lax.fori_loop(0, count, attend_group, 0)
-    for g in range(count):
-        departure(g).wait()
-
-
-def attend(queries, held, here, first=0, onto=None):
+    if first is not None:
+        for g in range(count):
+            departure(g).wait()
+
+
+def attend(queries, held, here, first=None, onto=None):
     rows = queries.shape[0]
     count = queries.shape[1] // WIDTH
     size = len(held)
     keys = size * rows
     so_far = [] if onto is None else [onto]
     hbm = pl.BlockSpec(memory_space=pl.ANY)
+    if first is None:
+        shape, place_spec = (count, rows, WIDTH), in_vmem(1)[0]
+        scratch = []
+    else:
+        shape, place_spec = (rows, KEY_VALUE_HEADS * WIDTH), hbm
+        scratch = [
+            pltpu.VMEM((count, rows, WIDTH), jnp.bfloat16),
+            pltpu.SemaphoreType.DMA((count,)),
+        ]
     return pl.pallas_call(
         functools.partial(attend_kernel, first, count, size),
         in_specs=[pl.BlockSpec(memory_space=pltpu.SMEM)] + in_vmem(1 + size) + [hbm] * len(so_far),
-        out_specs=hbm,
-        out_shape=jax.ShapeDtypeStruct((rows, KEY_VALUE_HEADS * WIDTH), jnp.bfloat16),
-        scratch_shapes=[
-            pltpu.VMEM((rows, keys), jnp.float32),
-            pltpu.VMEM((count, rows, WIDTH), jnp.bfloat16),
-            pltpu.SemaphoreType.DMA((count,)),
-        ],
+        out_specs=place_spec,
+        out_shape=jax.ShapeDtypeStruct(shape, jnp.bfloat16),
+        scratch_shapes=[pltpu.VMEM((rows, keys), jnp.float32), *scratch],
         input_output_aliases={2 + size: 0} if so_far else {},
         compiler_params=pltpu.CompilerParams(vmem_limit_bytes=(12 << 20) + 9216 * keys),
         name="attend",
@@ -262,7 +272,38 @@
             bytes_accessed=4 * rows * count * WIDTH,
             transcendentals=rows * keys * count * GROUP,
         ),
-    )(here, queries, *held, *so_far)
+    )(here, queries, *(map(kept_in_hbm, held) if first is None else held), *so_far)
+
+
+def place_kernel(count, block_ref, _, out_hbm, sems):
+    copies = [
+        pltpu.make_async_copy(
+            block_ref.at[g], out_hbm.at[:, head_columns(g, WIDTH)], sems.at[g]
+        )
+        for g in range(count)
+    ]
+    for copy in copies:
+        copy.start()
+    for copy in copies:
+        copy.wait()
+
+
+def place(block, onto):
+    count = block.shape[0]
+    hbm = pl.BlockSpec(memory_space=pl.ANY)
+    return pl.pallas_call(
+        functools.partial(place_kernel, count),
+        in_specs=in_vmem(1) + [hbm],
+        out_specs=hbm,
+        out_shape=jax.ShapeDtypeStruct(onto.shape, onto.dtype),
+        scratch_shapes=[pltpu.SemaphoreType.DMA((count,))],
+        input_output_aliases={1: 0},
+        compiler_params=pltpu.CompilerParams(vmem_limit_bytes=SMALL_LIMIT),
+        name="place",
+        cost_estimate=pl.CostEstimate(
+            flops=0, bytes_accessed=4 * block.size, transcendentals=0
+        ),
+    )(block, onto)
 
 
 def ring(block, axis):
@@ -290,20 +331,22 @@
     packed, tables = pack(CHUNKS, positions, segments, projected_keys[0], projected_values[0])
     held = []
     for c, payload in enumerate(packed):
-        blocks = [ring(payload, "pipe")]
+        blocks = [payload]
         for hop in range(1, size):
-            both = hop == 1 and c in DIAGONAL
+            both = hop == 1 and c > 0
             blocks.append(ring_both(payload) if both else ring(blocks[-1], "seq"))
+        if c > 0:
+            blocks[0] = ring(payload, "pipe")
         held.append(blocks)
     turned = rotate(CHUNKS, query_states[0], tables)
+    early = attend(turned[0], held[0], here)
+    early = ring(early, "pipe")
     out = None
-    for c in range(len(CHUNKS)):
+    for c in range(1, len(CHUNKS)):
         queries = ring(turned[c], "pipe")
         out = attend(queries, held[c], here, firsts[c], out)
+    out = place(early, out)
     return out[None]
-
-
-DIAGONAL = (0, 1, 2)
 
 
 def solution(mesh):

time: 63.6 us -> 65.8 us (1.035)
  waiting for transfers between devices: 29.7 us -> 34.7 us
  local copies, waits for them, and re-layouts: 6.22 us -> 2.49 us
  starting transfers between devices: 10.9 us -> 12.2 us
    ppermute x12, waiting for transfers between devices: 26.1 us -> 30.4 us  [ring(): return lax.ppermute(block, axis, [(i, (i + 1) % size) for i in range(size)])]
    unnamed x16 -> x12, local copies, waits for them, and re-layouts: 6.22 us -> 2.49 us
    ppermute x12, starting transfers between devices: 4.22 us -> 7.8 us  [ring(): return lax.ppermute(block, axis, [(i, (i + 1) % size) for i in range(size)])]
    ppermute x3 -> x2, starting transfers between devices: 6.68 us -> 4.45 us  [ring_both(): return lax.ppermute(block, ('pipe', 'seq'), route)]
    pallas_call x0 -> x1, Pallas kernels: none -> 0.81 us  [place(): pl.pallas_call(functools.partial(place_kernel, count), in_specs=in_vmem(1...]
    ppermute x3 -> x2, waiting for transfers between devices: 3.6 us -> 4.27 us  [ring_both(): return lax.ppermute(block, ('pipe', 'seq'), route)]
  transfers between devices with their start and end apart: 15 -> 14, of which waited for: 6 -> 8; matrix products, arithmetic and copies ran while one was open for 0% -> 0% of each run, Pallas kernels for 17% -> 20%
where the time goes in v1:
time: 65.8 us; the launch traced here: 65.5 us
  waiting for transfers between devices  34.7 us (53%)
  Pallas kernels  15.9 us (24%)
  starting transfers between devices  12.2 us (19%)
  local copies, waits for them, and re-layouts  2.49 us (4%)
    ppermute x12, waiting for transfers between devices, ring(): return lax.ppermute(block, axis, [(i, (i + 1) % size) for i in range(size)])  30.4 us
    pallas_call x3, Pallas kernels, attend(): pl.pallas_call(functools.partial(attend_kernel, first, count, size), in_s...  10 us
    ppermute x12, starting transfers between devices, ring(): return lax.ppermute(block, axis, [(i, (i + 1) % size) for i in range(size)])  7.8 us
    ppermute x2, starting transfers between devices, ring_both(): return lax.ppermute(block, ('pipe', 'seq'), route)  4.45 us
    ppermute x2, waiting for transfers between devices, ring_both(): return lax.ppermute(block, ('pipe', 'seq'), route)  4.27 us
    pallas_call x1, Pallas kernels, rotate(): pl.pallas_call(functools.partial(rotate_kernel, chunks), in_specs=in_vmem...  3.17 us
    unnamed x12, local copies, waits for them, and re-layouts  2.49 us
    pallas_call x1, Pallas kernels, pack(): pl.pallas_call(functools.partial(pack_kernel, chunks), in_specs=in_vmem(1...  1.94 us
  transfers between devices with their start and end apart: 14, of which 8 were waited for; matrix products, arithmetic and copies ran while one was open for 0% of the time, Pallas kernels for 20%

profile of v1, /device:TPU:0, one launch (start us, length us, event | category | flops | bytes accessed | tf_op | source)
XLA Modules:
  0.0 65.5 jit_solution(17861220823305305149)
XLA Ops:
  0.0 0.1 maximum_bitcast_fusion.rates_ref
  0.1 1.9 %pack.1 = (bf16[528,128]{1,0:T(8,128)(2,1)S(1)}, bf16[784,128]{1,0:T(8,128)(2,1)}, bf16[784,128]{1,0:T(8,128)(2,1)S(1)}, f32[128,128]{1,0:T(8,128)S(1)}, f32[128,128]{1,0:T(8,128)S(1)}) custom-call(f32[1,128]{1,0:T(1,128)S(1)} %maximum_bitcast_fusion.rates_ref, s32[1,128]{1,0:T(1,128)} %refs_0_.1, s32[1,128]{1,0:T(1,128)} %refs_1_.1, ...), custom_call_target="tpu_custom_call" | custom-call | flops 1048576 | bytes 1048576 | tf_op jit(solution)/shard_map/pack/pallas_call | solution.py:108
  2.0 3.1 %collective-permute-start = (bf16[528,128]{1,0:T(8,128)(2,1)S(1)}, bf16[528,128]{1,0:T(8,128)(2,1)S(1)}, u32[]{:S(2)}, u32[]{:S(2)}) collective-permute-start(bf16[528,128]{1,0:T(8,128)(2,1)S(1)} %get-tuple-element.16.refs_0_), channel_id=1, source_target_pairs={{0,1},{1,2},{2,3},{3,0},{4,5},{5,6},{6,7},{7,4},{8,9},{9,10},{10,1... | collective-permute-start | bytes 405512 | tf_op jit(solution)/shard_map/ppermute | solution.py:311
  5.2 5.6 %collective-permute-done.refs_1_ = bf16[528,128]{1,0:T(8,128)(2,1)S(1)} collective-permute-done((bf16[528,128]{1,0:T(8,128)(2,1)S(1)}, bf16[528,128]{1,0:T(8,128)(2,1)S(1)}, u32[]{:S(2)}, u32[]{:S(2)}) %collective-permute-start) | collective-permute-done | bytes 135200 | tf_op jit(solution)/shard_map/ppermute | solution.py:311
  10.8 0.0 collective-permute-start.1
  10.8 3.2 %rotate.1 = (bf16[128,2048]{1,0:T(8,128)(2,1)S(1)}, bf16[128,3072]{1,0:T(8,128)(2,1)}, bf16[128,3072]{1,0:T(8,128)(2,1)S(1)}) custom-call(f32[128,128]{1,0:T(8,128)S(1)} %get-tuple-element.13.cos_ref, f32[128,128]{1,0:T(8,128)S(1)} %get-tuple-element.14.sin_ref, bf16[128,8192]{1,0:T(8,128)(2,1)} %bitcast.7), custom_call_target="tpu_custom_call" | custom-call | flops 4194304 | bytes 4194304 | tf_op jit(solution)/shard_map/rotate/pallas_call | solution.py:148
  14.0 0.8 %copy-done = bf16[128,2048]{1,0:T(8,128)(2,1)} copy-done((bf16[128,2048]{1,0:T(8,128)(2,1)}, bf16[128,2048]{1,0:T(8,128)(2,1)S(1)}, u32[]{:S(2)}) %copy-start) | copy-done | bytes 524312
  14.8 0.0 collective-permute-start.9
  14.8 2.4 %collective-permute-start.11 = (bf16[784,128]{1,0:T(8,128)(2,1)}, bf16[784,128]{1,0:T(8,128)(2,1)S(1)}, u32[]{:S(2)}, u32[]{:S(2)}) collective-permute-start(bf16[784,128]{1,0:T(8,128)(2,1)} %get-tuple-element.20), channel_id=1, source_target_pairs={{0,5},{1,6},{2,7},{3,4},{4,9},{5,10},{6,11},{7,8},{8,13},{9,14},{1... | collective-permute-start | bytes 602120 | tf_op jit(solution)/shard_map/ppermute | solution.py:321
  17.2 0.4 collective-permute-done.1.refs_2_
  17.6 1.3 %collective-permute-start.2 = (bf16[528,128]{1,0:T(8,128)(2,1)S(1)}, bf16[528,128]{1,0:T(8,128)(2,1)S(1)}, u32[]{:S(2)}, u32[]{:S(2)}) collective-permute-start(bf16[528,128]{1,0:T(8,128)(2,1)S(1)} %collective-permute-done.1.refs_2_), channel_id=1, source_target_pairs={{0,1},{1,2},{2,3},{3,0},{4,5},{5,6},{6,7},{7,4},{8,9},{9,10},{10,1... | collective-permute-start | bytes 405512 | tf_op jit(solution)/shard_map/ppermute | solution.py:311
  18.8 2.0 %collective-permute-start.6 = (bf16[784,128]{1,0:T(8,128)(2,1)S(1)}, bf16[784,128]{1,0:T(8,128)(2,1)S(1)}, u32[]{:S(2)}, u32[]{:S(2)}) collective-permute-start(bf16[784,128]{1,0:T(8,128)(2,1)S(1)} %get-tuple-element.18), channel_id=1, source_target_pairs={{0,5},{1,6},{2,7},{3,4},{4,9},{5,10},{6,11},{7,8},{8,13},{9,14},{1... | collective-permute-start | bytes 602120 | tf_op jit(solution)/shard_map/ppermute | solution.py:321
  20.8 4.3 %collective-permute-done.11.refs_1_ = bf16[784,128]{1,0:T(8,128)(2,1)S(1)} collective-permute-done((bf16[784,128]{1,0:T(8,128)(2,1)}, bf16[784,128]{1,0:T(8,128)(2,1)S(1)}, u32[]{:S(2)}, u32[]{:S(2)}) %collective-permute-start.11) | collective-permute-done | bytes 200736 | tf_op jit(solution)/shard_map/ppermute | solution.py:321
  25.1 0.5 collective-permute-start.10
  25.7 3.1 %collective-permute-done.2.refs_3_ = bf16[528,128]{1,0:T(8,128)(2,1)S(1)} collective-permute-done((bf16[528,128]{1,0:T(8,128)(2,1)S(1)}, bf16[528,128]{1,0:T(8,128)(2,1)S(1)}, u32[]{:S(2)}, u32[]{:S(2)}) %collective-permute-start.2) | collective-permute-done | bytes 135200 | tf_op jit(solution)/shard_map/ppermute | solution.py:311
  28.7 0.6 copy-done.5
  29.4 0.0 collective-permute-start.12
  29.4 1.0 %copy-done.1 = bf16[128,2048]{1,0:T(8,128)(2,1)S(1)} copy-done((bf16[128,2048]{1,0:T(8,128)(2,1)S(1)}, bf16[128,2048]{1,0:T(8,128)(2,1)}, u32[]{:S(2)}) %copy-start.1) | copy-done | bytes 524312
  30.4 3.0 %attend.3 = bf16[2,128,1024]{2,1,0:T(8,128)(2,1)S(1)} custom-call(s32[1]{0:T(128)} %bitcast.here_ref, bf16[128,2048]{1,0:T(8,128)(2,1)S(1)} %copy-done.1, bf16[528,128]{1,0:T(8,128)(2,1)} %copy-done.2, bf16[528,128]{1,0:T(8,128)(2,1)} %copy-done.3, bf16[528,128]{1,0:T(8,128)(2,1)} %copy-done.4, bf16[528,128]{1,0:T(8,128)(2,1)} %copy-done.5), custom_call_target="tpu_custom_call" | custom-call | flops 536870912 | bytes 1048576 | tf_op jit(solution)/shard_map/attend/pallas_call | solution.py:261
  33.4 0.1 collective-permute-start.3
  33.5 7.8 %collective-permute-done.10.refs_0_ = bf16[784,128]{1,0:T(8,128)(2,1)S(1)} collective-permute-done((bf16[784,128]{1,0:T(8,128)(2,1)}, bf16[784,128]{1,0:T(8,128)(2,1)S(1)}, u32[]{:S(2)}, u32[]{:S(2)}) %collective-permute-start.10) | collective-permute-done | bytes 200736 | tf_op jit(solution)/shard_map/ppermute | solution.py:311
  41.3 1.2 %collective-permute-start.7 = (bf16[784,128]{1,0:T(8,128)(2,1)S(1)}, bf16[784,128]{1,0:T(8,128)(2,1)S(1)}, u32[]{:S(2)}, u32[]{:S(2)}) collective-permute-start(bf16[784,128]{1,0:T(8,128)(2,1)S(1)} %collective-permute-done.6.refs_1_), channel_id=1, source_target_pairs={{0,1},{1,2},{2,3},{3,0},{4,5},{5,6},{6,7},{7,4},{8,9},{9,10},{10,1... | collective-permute-start | bytes 602120 | tf_op jit(solution)/shard_map/ppermute | solution.py:311
  42.5 0.0 collective-permute-done.12.refs_2_
  42.5 1.6 %collective-permute-start.13 = (bf16[784,128]{1,0:T(8,128)(2,1)S(1)}, bf16[784,128]{1,0:T(8,128)(2,1)S(1)}, u32[]{:S(2)}, u32[]{:S(2)}) collective-permute-start(bf16[784,128]{1,0:T(8,128)(2,1)S(1)} %collective-permute-done.12.refs_2_), channel_id=1, source_target_pairs={{0,1},{1,2},{2,3},{3,0},{4,5},{5,6},{6,7},{7,4},{8,9},{9,10},{10,1... | collective-permute-start | bytes 602120 | tf_op jit(solution)/shard_map/ppermute | solution.py:311
  44.1 6.8 %collective-permute-done.7.refs_2_ = bf16[784,128]{1,0:T(8,128)(2,1)S(1)} collective-permute-done((bf16[784,128]{1,0:T(8,128)(2,1)S(1)}, bf16[784,128]{1,0:T(8,128)(2,1)S(1)}, u32[]{:S(2)}, u32[]{:S(2)}) %collective-permute-start.7) | collective-permute-done | bytes 200736 | tf_op jit(solution)/shard_map/ppermute | solution.py:311
  50.9 0.0 collective-permute-start.5
  50.9 2.8 %collective-permute-done.13.refs_3_ = bf16[784,128]{1,0:T(8,128)(2,1)S(1)} collective-permute-done((bf16[784,128]{1,0:T(8,128)(2,1)S(1)}, bf16[784,128]{1,0:T(8,128)(2,1)S(1)}, u32[]{:S(2)}, u32[]{:S(2)}) %collective-permute-start.13) | collective-permute-done | bytes 200736 | tf_op jit(solution)/shard_map/ppermute | solution.py:311
  53.7 0.0 collective-permute-start.8
  53.7 3.5 %attend.4.refs_4_ = bf16[128,8192]{1,0:T(8,128)(2,1)} custom-call(s32[1]{0:T(128)} %bitcast.here_ref, bf16[128,3072]{1,0:T(8,128)(2,1)S(1)} %collective-permute-done.9.queries_ref, bf16[784,128]{1,0:T(8,128)(2,1)S(1)} %collective-permute-done.10.refs_0_, bf16[784,128]{1,0:T(8,128)(2,1)S(1)} %collective-permute-done.11.refs_1_, ...), custom_call_target="tpu_custom_call" | custom-call | flops 805306368 | bytes 1572864 | tf_op jit(solution)/shard_map/attend/pallas_call | solution.py:261
  57.3 3.9 %collective-permute-done.8.refs_3_ = bf16[784,128]{1,0:T(8,128)(2,1)S(1)} collective-permute-done((bf16[784,128]{1,0:T(8,128)(2,1)S(1)}, bf16[784,128]{1,0:T(8,128)(2,1)S(1)}, u32[]{:S(2)}, u32[]{:S(2)}) %collective-permute-start.8) | collective-permute-done | bytes 200736 | tf_op jit(solution)/shard_map/ppermute | solution.py:311
  61.2 3.5 %attend.5._ = bf16[128,8192]{1,0:T(8,128)(2,1)} custom-call(s32[1]{0:T(128)} %bitcast.here_ref, bf16[128,3072]{1,0:T(8,128)(2,1)S(1)} %collective-permute-done.4.queries_ref, bf16[784,128]{1,0:T(8,128)(2,1)S(1)} %collective-permute-done.5.refs_0_, bf16[784,128]{1,0:T(8,128)(2,1)S(1)} %collective-permute-done.6.refs_1_, ...), custom_call_target="tpu_custom_call", output_to_operand_aliasing={{}: (6, {})} | custom-call | flops 805306368 | bytes 1572864 | tf_op jit(solution)/shard_map/attend/pallas_call | solution.py:261
  64.7 0.8 %place.1 = bf16[128,8192]{1,0:T(8,128)(2,1)} custom-call(bf16[2,128,1024]{2,1,0:T(8,128)(2,1)S(1)} %collective-permute-done.3.block_ref, bf16[128,8192]{1,0:T(8,128)(2,1)} %attend.5._), custom_call_target="tpu_custom_call", output_to_operand_aliasing={{}: (1, {})} | custom-call | bytes 1048576 | tf_op jit(solution)/shard_map/place/pallas_call | solution.py:294
  (16 shorter events, 0.0 us)
Async XLA Ops:
  2.0 27.3 %copy-start.2 = (bf16[528,128]{1,0:T(8,128)(2,1)}, bf16[528,128]{1,0:T(8,128)(2,1)S(1)}, u32[]{:S(2)}) copy-start(bf16[528,128]{1,0:T(8,128)(2,1)S(1)} %get-tuple-element.16.refs_0_) | copy-start | bytes 405508
  2.0 8.7 %collective-permute-start = (bf16[528,128]{1,0:T(8,128)(2,1)S(1)}, bf16[528,128]{1,0:T(8,128)(2,1)S(1)}, u32[]{:S(2)}, u32[]{:S(2)}) collective-permute-start(bf16[528,128]{1,0:T(8,128)(2,1)S(1)} %get-tuple-element.16.refs_0_), channel_id=1, source_target_pairs={{0,1},{1,2},{2,3},{3,0},{4,5},{5,6},{6,7},{7,4},{8,9},{9,10},{10,1... | collective-permute-start | bytes 405512 | tf_op jit(solution)/shard_map/ppermute | solution.py:311
  10.8 8.1 %copy-start.3 = (bf16[528,128]{1,0:T(8,128)(2,1)}, bf16[528,128]{1,0:T(8,128)(2,1)S(1)}, u32[]{:S(2)}) copy-start(bf16[528,128]{1,0:T(8,128)(2,1)S(1)} %collective-permute-done.refs_1_) | copy-start | bytes 405508
  10.8 6.8 %collective-permute-start.1 = (bf16[528,128]{1,0:T(8,128)(2,1)S(1)}, bf16[528,128]{1,0:T(8,128)(2,1)S(1)}, u32[]{:S(2)}, u32[]{:S(2)}) collective-permute-start(bf16[528,128]{1,0:T(8,128)(2,1)S(1)} %collective-permute-done.refs_1_), channel_id=1, source_target_pairs={{0,1},{1,2},{2,3},{3,0},{4,5},{5,6},{6,7},{7,4},{8,9},{9,10},{10,1... | collective-permute-start | bytes 405512 | tf_op jit(solution)/shard_map/ppermute | solution.py:311
  13.9 0.8 %copy-start = (bf16[128,2048]{1,0:T(8,128)(2,1)}, bf16[128,2048]{1,0:T(8,128)(2,1)S(1)}, u32[]{:S(2)}) copy-start(bf16[128,2048]{1,0:T(8,128)(2,1)S(1)} %get-tuple-element.15.queries_ref) | copy-start | bytes 1572868
  14.8 39.0 %collective-permute-start.9 = (bf16[128,3072]{1,0:T(8,128)(2,1)}, bf16[128,3072]{1,0:T(8,128)(2,1)S(1)}, u32[]{:S(2)}, u32[]{:S(2)}) collective-permute-start(bf16[128,3072]{1,0:T(8,128)(2,1)} %get-tuple-element.19), channel_id=1, source_target_pairs={{0,4},{4,8},{8,12},{12,0},{1,5},{5,9},{9,13},{13,1},{2,6},{6,10},{... | collective-permute-start | bytes 2359304 | tf_op jit(solution)/shard_map/ppermute | solution.py:311
  14.8 10.4 %collective-permute-start.11 = (bf16[784,128]{1,0:T(8,128)(2,1)}, bf16[784,128]{1,0:T(8,128)(2,1)S(1)}, u32[]{:S(2)}, u32[]{:S(2)}) collective-permute-start(bf16[784,128]{1,0:T(8,128)(2,1)} %get-tuple-element.20), channel_id=1, source_target_pairs={{0,5},{1,6},{2,7},{3,4},{4,9},{5,10},{6,11},{7,8},{8,13},{9,14},{1... | collective-permute-start | bytes 602120 | tf_op jit(solution)/shard_map/ppermute | solution.py:321
  17.2 44.0 %collective-permute-start.4 = (bf16[128,3072]{1,0:T(8,128)(2,1)S(1)}, bf16[128,3072]{1,0:T(8,128)(2,1)S(1)}, u32[]{:S(2)}, u32[]{:S(2)}) collective-permute-start(bf16[128,3072]{1,0:T(8,128)(2,1)S(1)} %get-tuple-element.17), channel_id=1, source_target_pairs={{0,4},{4,8},{8,12},{12,0},{1,5},{5,9},{9,13},{13,1},{2,6},{6,10},{... | collective-permute-start | bytes 2359304 | tf_op jit(solution)/shard_map/ppermute | solution.py:311
  17.6 8.1 %copy-start.4 = (bf16[528,128]{1,0:T(8,128)(2,1)}, bf16[528,128]{1,0:T(8,128)(2,1)S(1)}, u32[]{:S(2)}) copy-start(bf16[528,128]{1,0:T(8,128)(2,1)S(1)} %collective-permute-done.1.refs_2_) | copy-start | bytes 405508
  17.6 11.2 %collective-permute-start.2 = (bf16[528,128]{1,0:T(8,128)(2,1)S(1)}, bf16[528,128]{1,0:T(8,128)(2,1)S(1)}, u32[]{:S(2)}, u32[]{:S(2)}) collective-permute-start(bf16[528,128]{1,0:T(8,128)(2,1)S(1)} %collective-permute-done.1.refs_2_), channel_id=1, source_target_pairs={{0,1},{1,2},{2,3},{3,0},{4,5},{5,6},{6,7},{7,4},{8,9},{9,10},{10,1... | collective-permute-start | bytes 405512 | tf_op jit(solution)/shard_map/ppermute | solution.py:311
  18.8 14.6 %collective-permute-start.6 = (bf16[784,128]{1,0:T(8,128)(2,1)S(1)}, bf16[784,128]{1,0:T(8,128)(2,1)S(1)}, u32[]{:S(2)}, u32[]{:S(2)}) collective-permute-start(bf16[784,128]{1,0:T(8,128)(2,1)S(1)} %get-tuple-element.18), channel_id=1, source_target_pairs={{0,5},{1,6},{2,7},{3,4},{4,9},{5,10},{6,11},{7,8},{8,13},{9,14},{1... | collective-permute-start | bytes 602120 | tf_op jit(solution)/shard_map/ppermute | solution.py:321
  25.1 16.1 %collective-permute-start.10 = (bf16[784,128]{1,0:T(8,128)(2,1)}, bf16[784,128]{1,0:T(8,128)(2,1)S(1)}, u32[]{:S(2)}, u32[]{:S(2)}) collective-permute-start(bf16[784,128]{1,0:T(8,128)(2,1)} %get-tuple-element.20), channel_id=1, source_target_pairs={{0,4},{4,8},{8,12},{12,0},{1,5},{5,9},{9,13},{13,1},{2,6},{6,10},{... | collective-permute-start | bytes 602120 | tf_op jit(solution)/shard_map/ppermute | solution.py:311
  28.7 0.6 copy-start.5
  29.4 13.1 %collective-permute-start.12 = (bf16[784,128]{1,0:T(8,128)(2,1)S(1)}, bf16[784,128]{1,0:T(8,128)(2,1)S(1)}, u32[]{:S(2)}, u32[]{:S(2)}) collective-permute-start(bf16[784,128]{1,0:T(8,128)(2,1)S(1)} %collective-permute-done.11.refs_1_), channel_id=1, source_target_pairs={{0,1},{1,2},{2,3},{3,0},{4,5},{5,6},{6,7},{7,4},{8,9},{9,10},{10,1... | collective-permute-start | bytes 602120 | tf_op jit(solution)/shard_map/ppermute | solution.py:311
  29.4 1.0 %copy-start.1 = (bf16[128,2048]{1,0:T(8,128)(2,1)S(1)}, bf16[128,2048]{1,0:T(8,128)(2,1)}, u32[]{:S(2)}) copy-start(bf16[128,2048]{1,0:T(8,128)(2,1)} %copy-done) | copy-start | bytes 1572868
  33.4 31.3 %collective-permute-start.3 = (bf16[2,128,1024]{2,1,0:T(8,128)(2,1)S(1)}, bf16[2,128,1024]{2,1,0:T(8,128)(2,1)S(1)}, u32[]{:S(2)}, u32[]{:S(2)}) collective-permute-start(bf16[2,128,1024]{2,1,0:T(8,128)(2,1)S(1)} %attend.3), channel_id=1, source_target_pairs={{0,4},{4,8},{8,12},{12,0},{1,5},{5,9},{9,13},{13,1},{2,6},{6,10},{... | collective-permute-start | bytes 1572872 | tf_op jit(solution)/shard_map/ppermute | solution.py:311
  41.3 9.7 %collective-permute-start.7 = (bf16[784,128]{1,0:T(8,128)(2,1)S(1)}, bf16[784,128]{1,0:T(8,128)(2,1)S(1)}, u32[]{:S(2)}, u32[]{:S(2)}) collective-permute-start(bf16[784,128]{1,0:T(8,128)(2,1)S(1)} %collective-permute-done.6.refs_1_), channel_id=1, source_target_pairs={{0,1},{1,2},{2,3},{3,0},{4,5},{5,6},{6,7},{7,4},{8,9},{9,10},{10,1... | collective-permute-start | bytes 602120 | tf_op jit(solution)/shard_map/ppermute | solution.py:311
  42.5 11.2 %collective-permute-start.13 = (bf16[784,128]{1,0:T(8,128)(2,1)S(1)}, bf16[784,128]{1,0:T(8,128)(2,1)S(1)}, u32[]{:S(2)}, u32[]{:S(2)}) collective-permute-start(bf16[784,128]{1,0:T(8,128)(2,1)S(1)} %collective-permute-done.12.refs_2_), channel_id=1, source_target_pairs={{0,1},{1,2},{2,3},{3,0},{4,5},{5,6},{6,7},{7,4},{8,9},{9,10},{10,1... | collective-permute-start | bytes 602120 | tf_op jit(solution)/shard_map/ppermute | solution.py:311
  50.9 6.4 %collective-permute-start.5 = (bf16[784,128]{1,0:T(8,128)(2,1)S(1)}, bf16[784,128]{1,0:T(8,128)(2,1)S(1)}, u32[]{:S(2)}, u32[]{:S(2)}) collective-permute-start(bf16[784,128]{1,0:T(8,128)(2,1)S(1)} %get-tuple-element.18), channel_id=1, source_target_pairs={{0,4},{4,8},{8,12},{12,0},{1,5},{5,9},{9,13},{13,1},{2,6},{6,10},{... | collective-permute-start | bytes 602120 | tf_op jit(solution)/shard_map/ppermute | solution.py:311
  53.7 7.5 %collective-permute-start.8 = (bf16[784,128]{1,0:T(8,128)(2,1)S(1)}, bf16[784,128]{1,0:T(8,128)(2,1)S(1)}, u32[]{:S(2)}, u32[]{:S(2)}) collective-permute-start(bf16[784,128]{1,0:T(8,128)(2,1)S(1)} %collective-permute-done.7.refs_2_), channel_id=1, source_target_pairs={{0,1},{1,2},{2,3},{3,0},{4,5},{5,6},{6,7},{7,4},{8,9},{9,10},{10,1... | collective-permute-start | bytes 602120 | tf_op jit(solution)/shard_map/ppermute | solution.py:311
